TPU v7x, 32 devices: a whole 2x2x4 slice. The times are simulated.
32 devices in a mesh: tiles: 2 (over x), morton: 16 (over z, y, core).
Axes of the slice: x: 2, y: 2, z: 4, core: 2. Of those that a mesh axis runs over, the one named last changes fastest.
Arguments:
- features: bfloat16 [256, 512, 64], P(('tiles', 'morton')), parts along dimension 0, may hold values from -6 to 6
- neighbours: int32 [256, 27], P(('tiles', 'morton')), parts along dimension 0, may hold values from -1 to 127, as said below
- occupancy: int32 [256, 16], P(('tiles', 'morton')), parts along dimension 0, may hold values from -2147483648 to 2147483647, as said below
- conv_one: bfloat16 [27, 64, 64], replicated, may hold values from -0.21875 to 0.21875
- first_reduce_kernel: bfloat16 [8, 64, 128], replicated, may hold values from -0.5 to 0.5
- conv_two: bfloat16 [27, 128, 128], replicated, may hold values from -0.1875 to 0.1875
- second_reduce_kernel: bfloat16 [8, 128, 256], replicated, may hold values from -0.375 to 0.375
- conv_three: bfloat16 [27, 256, 256], replicated, may hold values from -0.125 to 0.125
Outputs:
- first_level_features: bfloat16 [256, 512, 64], P(('tiles', 'morton')), parts along dimension 0
- second_level_features: bfloat16 [256, 64, 128], P(('tiles', 'morton')), parts along dimension 0
- skip_three: bfloat16 [256, 8, 256], P(('tiles', 'morton')), parts along dimension 0
There are 2 independent parts, one for each index of `tiles`. A program takes and returns all parts, laid end to end along the dimension named above; an argument that names none is the same for every part. Nothing has to cross between parts.
Inputs may be any that keep to these rules, and one draw needn't show every extreme that they name: `neighbours`: bricks are numbered by x slice, then by cell of the slice's 4 x 4 cross-section in rising order, 8 occupied bricks to a slice. Entry 9 (a+1) + 3 (c+1) + (e+1) of a brick's row is the number of the brick at offset (a, c, e), or -1 if that cell is empty or outside the tile; entry 13 is the brick itself. Every neighbour lies in the brick's own slice or in an adjacent one. Bit k, the lowest being bit 0, of word w of a brick's row is the occupancy of voxel 32 w + k; bit 31 is the sign bit of the word.
All inputs are finite; a program needn't handle non-finite values.
Results may differ from a plain program's by a relative error of at most 0.008.
Values may be sent and summed in bfloat16 or wider, within the bound.
A program may use at most 128 MiB of HBM per device.

v0:
```python
import jax
import jax.numpy as jnp
from jax import lax
from jax.experimental import pallas as pl
from jax.experimental.pallas import tpu as pltpu
from jax.sharding import PartitionSpec as P

BRICKS = 8
LANES = 512
F32 = jnp.float32
BF16 = jnp.bfloat16


def iota(shape, dim):
    return lax.broadcasted_iota(jnp.int32, shape, dim)


def band_pairs(source, band):
    @pl.loop(0, 9)
    def _(tap):
        minus, same, plus = (source[3 * tap + e] for e in range(3))
        zero = jnp.zeros_like(same)
        low = jnp.concatenate([same, minus], axis=1)
        high = jnp.concatenate([plus, same], axis=1)
        before = jnp.concatenate([minus, zero], axis=1)
        after = jnp.concatenate([zero, plus], axis=1)
        blank = jnp.zeros((64, 128), BF16)
        rows = (
            (blank, blank), (before, blank),
            (low, blank), (high, before),
            (after, low), (blank, high),
            (blank, after), (blank, blank),
        )
        for at, (left, right) in enumerate(rows):
            band[tap, at * 64 : at * 64 + 64, 0:128] = left
            band[tap, at * 64 : at * 64 + 64, 128:256] = right


def band_single(source, band):
    @pl.loop(0, 9)
    def _(tap):
        minus, same, plus = (source[3 * tap + e] for e in range(3))
        blank = jnp.zeros_like(same)
        rows = ((minus, blank), (same, minus), (plus, same), (blank, plus))
        for at, (left, right) in enumerate(rows):
            band[tap, at * 128 : at * 128 + 128, 0:128] = left
            band[tap, at * 128 : at * 128 + 128, 128:256] = right


def assemble(side, halo, nb, own, low, high, cols):
    row = iota((8, LANES + 2 * halo), 0)

    def source(brick, tap):
        number = nb[brick, tap]
        return jnp.where(number < 0, BRICKS, lax.rem(number, BRICKS))

    @pl.loop(0, BRICKS // 2)
    def _(pair):
        for dx, ref in ((0, low), (1, own), (2, high)):
            index = [
                [[source(2 * pair + b, 9 * dx + 3 * dy + dz) for dz in range(3)] for dy in range(3)]
                for b in range(2)
            ]
            for plane in range(side if dx == 1 else 1):
                at = slice(8 * plane, 8 * plane + 8)
                shifted = [[], [], []]
                for b in range(2):
                    views = []
                    for dy in range(3):
                        before, here, after = index[b][dy]
                        views.append(
                            jnp.concatenate(
                                [
                                    ref[before, at, LANES - halo : LANES],
                                    ref[here, at, :],
                                    ref[after, at, 0:halo],
                                ],
                                axis=1,
                            )
                        )
                    back, mid, front = views
                    shifted[0].append(
                        jnp.where(
                            row == 0,
                            pltpu.roll(back, (9 - side) % 8, 0),
                            pltpu.roll(mid, 1, 0),
                        )
                    )
                    shifted[1].append(mid)
                    shifted[2].append(
                        jnp.where(
                            row == side - 1,
                            pltpu.roll(front, side - 1, 0),
                            pltpu.roll(mid, 7, 0),
                        )
                    )
                to = plane + 1 if dx == 1 else (0 if dx == 0 else side + 1)
                rows = pl.ds(pl.multiple_of(16 * pair, 16), 16)
                for c in range(3):
                    cols[c, to, rows, :] = jnp.concatenate(shifted[c], axis=0).astype(BF16)


def convolve(side, depth, cols, weights, finish):
    chunk = min(side, 4)
    matrix = jnp.concatenate([weights(tap) for tap in range(9)], axis=0)
    for half in range(2):
        lanes = slice(256 * half, 256 * half + depth)
        for first in range(0, side, chunk):
            left = jnp.concatenate(
                [
                    cols[c, first + a : first + a + chunk, :, lanes].reshape(chunk * 64, depth)
                    for a in range(3)
                    for c in range(3)
                ],
                axis=1,
            )
            sums = jnp.dot(left, matrix, preferred_element_type=F32)
            finish(half, first, sums.reshape(chunk, BRICKS, 8, 256))


def rounded(value):
    return value.astype(BF16).astype(F32)


def pool_bits(bits, fine_side, temp, pooled):
    half = fine_side // 2
    count = BRICKS * half * 8
    joined = bits[0 : BRICKS * fine_side * 8, :].reshape(BRICKS * half, 2, 8, 128)
    temp[0:count, :] = (joined[:, 0] | joined[:, 1]).reshape(count, 128)
    temp[count : count + 16, :] = jnp.zeros((16, 128), jnp.int32)
    for at in range(BRICKS * half):
        even = temp[pl.ds(8 * at, 8, stride=2), :]
        odd = temp[pl.ds(8 * at + 1, 8, stride=2), :]
        pooled[8 * at : 8 * at + 8, :] = even | odd


def reduce_level(side, block, fine, kernel, bits, bit_width, emit):
    half = side // 2
    width = 2 * block
    for at in range(LANES // width):
        parts = []
        for ci in range(2):
            for cj in range(2):
                pieces = []
                for lane in range(at * width, (at + 1) * width, 128):
                    pieces.append(
                        jnp.concatenate(
                            [
                                fine[lane // 128, pl.ds((b * side + 2 * i + ci) * 8 + cj, 8, stride=2), :]
                                for b in range(BRICKS)
                                for i in range(half)
                            ],
                            axis=0,
                        )
                    )
                parts += pieces
        left = jnp.concatenate(parts, axis=1).astype(BF16)
        sums = jnp.dot(left, kernel, preferred_element_type=F32)
        mask = ((bits[0 : BRICKS * half * 8, :] >> (bit_width * at)) & ((1 << bit_width) - 1)) != 0
        wide = sums.shape[1]
        for lane in range(0, wide, 128):
            emit(
                at * wide + lane,
                jnp.where(mask, jnp.maximum(sums[:, lane : lane + 128], 0.0), 0.0),
            )


def level_one(nb, feat, occ, low_in, high_in, weights, kernel,
              out, next_own, next_low, next_high, next_bits,
              own, low, high, cols, band, fine, temp, wide, bits, bits_temp):
    band_pairs(weights, band)
    lane = iota((64, 128), 1)
    row = iota((64, 16), 0)
    column = iota((64, 16), 1)
    upper = (lane >= 64).astype(jnp.int32)
    own[BRICKS] = jnp.zeros((64, LANES), F32)
    low[BRICKS] = jnp.zeros((8, LANES), F32)
    high[BRICKS] = jnp.zeros((8, LANES), F32)

    @pl.loop(0, BRICKS)
    def _(b):
        words = jnp.broadcast_to(occ[pl.ds(b, 1), :], (64, 16))
        octet = (words >> (8 * (row % 4))) & 255
        picked = jnp.where(column == row // 4, octet.astype(F32), 0.0)
        mask = jnp.broadcast_to(jnp.sum(picked, axis=1, keepdims=True), (64, 128)).astype(jnp.int32)
        bits[pl.ds(pl.multiple_of(64 * b, 64), 64), :] = mask
        temp[:, 0:64] = feat[b].astype(F32)
        for q in range(4):
            even = temp[pl.ds(2 * q, 64, stride=8), :]
            odd = temp[pl.ds(2 * q + 1, 64, stride=8), :]
            both = jnp.where(lane < 64, even, pltpu.roll(odd, 64, 1))
            own[b, :, 128 * q : 128 * q + 128] = jnp.where(
                ((mask >> (2 * q + upper)) & 1) != 0, both, 0.0
            )
    for ref, source in ((low, low_in), (high, high_in)):
        temp[:, 0:64] = source[...].astype(F32).reshape(512, 64)
        for q in range(4):
            even = temp[pl.ds(2 * q, 64, stride=8), :]
            odd = temp[pl.ds(2 * q + 1, 64, stride=8), :]
            both = jnp.where(lane < 64, even, pltpu.roll(odd, 64, 1))
            ref[0:BRICKS, :, 128 * q : 128 * q + 128] = both.reshape(BRICKS, 8, 128)

    assemble(8, 128, nb, own, low, high, cols)
    small = iota((8, 128), 1)
    small_upper = (small >= 64).astype(jnp.int32)

    def finish(half, first, sums):
        for p in range(sums.shape[0]):
            for b in range(BRICKS):
                at = b * 64 + (first + p) * 8
                mask = bits[at : at + 8, :]
                for part in range(2):
                    q = 2 * half + part
                    fine[q, at : at + 8, :] = rounded(
                        jnp.where(
                            ((mask >> (2 * q + small_upper)) & 1) != 0,
                            jnp.maximum(sums[p, b, :, 128 * part : 128 * part + 128], 0.0),
                            0.0,
                        )
                    )

    convolve(8, 512, cols, lambda tap: band[tap], finish)
    fine[:, 512:528, :] = jnp.zeros((4, 16, 128), F32)
    pool_bits(bits, 8, bits_temp, next_bits)

    def emit(lane_at, value):
        value = value.reshape(BRICKS, 32, 128)
        lanes = slice(lane_at, lane_at + 128)
        next_own[:, :, lanes] = value
        next_low[:, :, lanes] = value[:, 0:8].astype(BF16)
        next_high[:, :, lanes] = value[:, 24:32].astype(BF16)

    reduce_level(8, 64, fine, kernel[...], next_bits, 2, emit)

    @pl.loop(0, BRICKS)
    def _(b):
        for q in range(4):
            both = fine[q, pl.ds(pl.multiple_of(64 * b, 64), 64), :]
            wide[pl.ds(2 * q, 64, stride=8), :] = both
            wide[pl.ds(2 * q + 1, 64, stride=8), :] = pltpu.roll(both, 64, 1)
        out[b] = wide[:, 0:64].astype(BF16)


def fill(own, low, high, own_in, low_in, high_in):
    own[0:BRICKS] = rounded(own_in[...])
    low[0:BRICKS] = low_in[...].astype(F32)
    high[0:BRICKS] = high_in[...].astype(F32)
    for ref in (own, low, high):
        ref[BRICKS] = jnp.zeros(ref.shape[1:], F32)


def level_two(nb, own_in, low_in, high_in, bits, weights, kernel,
              out, next_own, next_low, next_high, next_bits,
              own, low, high, cols, band, fine, wide, bits_temp):
    band_single(weights, band)
    fill(own, low, high, own_in, low_in, high_in)
    assemble(4, 128, nb, own, low, high, cols)

    def finish(half, first, sums):
        for p in range(sums.shape[0]):
            for b in range(BRICKS):
                at = b * 32 + (first + p) * 8
                mask = bits[at : at + 8, :]
                for part in range(2):
                    q = 2 * half + part
                    fine[q, at : at + 8, :] = rounded(
                        jnp.where(
                            ((mask >> (2 * q)) & 3) != 0,
                            jnp.maximum(sums[p, b, :, 128 * part : 128 * part + 128], 0.0),
                            0.0,
                        )
                    )

    convolve(4, 512, cols, lambda tap: band[tap], finish)
    fine[:, 256:272, :] = jnp.zeros((4, 16, 128), F32)
    pool_bits(bits, 4, bits_temp, next_bits)

    def emit(lane_at, value):
        value = value.reshape(BRICKS, 16, 128)
        lanes = slice(lane_at, lane_at + 128)
        next_own[:, :, lanes] = value
        next_low[:, :, lanes] = value[:, 0:8].astype(BF16)
        next_high[:, :, lanes] = value[:, 8:16].astype(BF16)

    reduce_level(4, 128, fine, kernel[...], next_bits, 4, emit)
    for b in range(BRICKS):
        for i in range(4):
            for k in range(4):
                at = b * 32 + 8 * i
                wide[pl.ds(64 * b + 16 * i + k, 4, stride=4), :] = fine[k, at : at + 4, :]
    out[...] = wide[...].reshape(BRICKS, 64, 128).astype(BF16)


def level_three(nb, own_in, low_in, high_in, bits, weights,
                out, own, low, high, cols, wide):
    fill(own, low, high, own_in, low_in, high_in)
    assemble(2, 256, nb, own, low, high, cols)

    def finish(half, first, sums):
        for p in range(sums.shape[0]):
            for b in range(BRICKS):
                at = b * 16 + (first + p) * 8
                mask = ((bits[at : at + 8, :] >> (4 * half)) & 15) != 0
                for part in range(2):
                    value = jnp.where(
                        mask, jnp.maximum(sums[p, b, :, 128 * part : 128 * part + 128], 0.0), 0.0
                    )
                    wide[part, pl.ds(8 * b + 4 * (first + p) + half, 2, stride=2), :] = value[0:2]

    convolve(2, 768, cols, lambda tap: weights[3 * tap : 3 * tap + 3].reshape(768, 256), finish)
    for part in range(2):
        out[:, :, 128 * part : 128 * part + 128] = wide[part].reshape(BRICKS, 8, 128).astype(BF16)


VM = pl.BlockSpec(memory_space=pltpu.VMEM)
SM = pl.BlockSpec(memory_space=pltpu.SMEM)


def call(body, outs, scratch, *args):
    return pl.pallas_call(
        body,
        out_shape=[jax.ShapeDtypeStruct(shape, dtype) for shape, dtype in outs],
        in_specs=[SM] + [VM] * (len(args) - 1),
        out_specs=[VM] * len(outs),
        scratch_shapes=[pltpu.VMEM(shape, dtype) for shape, dtype in scratch],
        compiler_params=pltpu.CompilerParams(vmem_limit_bytes=56 << 20),
    )(*args)


def exchange(first, last):
    count = lax.axis_size("morton")
    forward = [(i, i + 1) for i in range(count - 1)]
    low = lax.ppermute(last, "morton", forward)
    high = lax.ppermute(first, "morton", [(b, a) for a, b in forward])
    return low, high


def volume(side, width):
    return [
        ((BRICKS + 1, side * 8, LANES), F32),
        ((BRICKS + 1, 8, LANES), F32),
        ((BRICKS + 1, 8, LANES), F32),
        ((3, side + 2, 64, width), BF16),
    ]


def masked_plane(features, occupancy, plane):
    words = occupancy[:, 2 * plane : 2 * plane + 2]
    bits = (words[:, :, None] >> jnp.arange(32, dtype=jnp.int32)) & 1
    values = features[:, 64 * plane : 64 * plane + 64, :]
    return jnp.where(bits.reshape(BRICKS, 64, 1) != 0, values, jnp.zeros((), BF16))


def on_device(features, neighbours, occupancy, conv_one, first_reduce_kernel,
              conv_two, second_reduce_kernel, conv_three):
    low, high = exchange(
        masked_plane(features, occupancy, 0), masked_plane(features, occupancy, 7)
    )
    band = [((9, 512, 256), BF16)]
    first, own, to_low, to_high, bits = call(
        level_one,
        [(features.shape, BF16), ((BRICKS, 32, LANES), F32), ((BRICKS, 8, LANES), BF16),
         ((BRICKS, 8, LANES), BF16), ((BRICKS * 32, 128), jnp.int32)],
        volume(8, 768) + band + [((4, 528, 128), F32), ((512, 128), F32), ((512, 128), F32),
                                 ((512, 128), jnp.int32), ((272, 128), jnp.int32)],
        neighbours, features, occupancy, low, high, conv_one,
        first_reduce_kernel.reshape(512, 128),
    )
    low, high = exchange(to_low, to_high)
    second, own, to_low, to_high, bits = call(
        level_two,
        [((BRICKS, 64, 128), BF16), ((BRICKS, 16, LANES), F32), ((BRICKS, 8, LANES), BF16),
         ((BRICKS, 8, LANES), BF16), ((BRICKS * 16, 128), jnp.int32)],
        volume(4, 768) + band + [((4, 272, 128), F32), ((512, 128), F32), ((144, 128), jnp.int32)],
        neighbours, own, low, high, bits, conv_two, second_reduce_kernel.reshape(1024, 256),
    )
    low, high = exchange(to_low, to_high)
    (third,) = call(
        level_three,
        [((BRICKS, 8, 256), BF16)],
        volume(2, 1024) + [((2, 64, 128), F32)],
        neighbours, own, low, high, bits, conv_three,
    )
    return first, second, third


def solution(mesh):
    split = P(("tiles", "morton"), None, None)
    flat = P(("tiles", "morton"), None)
    return jax.shard_map(
        on_device,
        mesh=mesh,
        in_specs=(split, flat, flat, P(), P(), P(), P(), P()),
        out_specs=(split, split, split),
        check_vma=False,
    )
```

profile of v0, /device:TPU:7, one launch (start us, length us, event | category | flops | bytes accessed | tf_op | source)
XLA Modules:
  0.0 53.6 jit_solution(12183743292679612804)
XLA Ops:
  0.6 0.1 shift_right_arithmetic.51
  0.7 0.8 %fusion = (s32[8,2]{1,0:T(8,128)S(1)}, s32[8,2]{1,0:T(8,128)S(1)}) fusion(s32[8,16]{1,0:T(8,128)} %occ.1), kind=kLoop, calls=%fused_computation.4 | loop fusion | bytes 256 | tf_op jit(solution)/shard_map/slice | solution.py:348
  1.6 0.1 shift_right_arithmetic.54
  1.6 0.1 shift_right_arithmetic.55
  1.8 0.1 shift_right_arithmetic.49
  1.9 1.5 %copy.13.feat = bf16[8,512,64]{2,1,0:T(8,128)(2,1)S(1)} copy(bf16[8,512,64]{1,2,0:T(8,128)(2,1)} %param.8) | data formatting | bytes 1048576 | tf_op args[0]
  3.4 0.2 slice_select_fusion
  3.6 2.6 %collective-permute-start.1 = (bf16[8,64,64]{2,1,0:T(8,128)(2,1)S(1)}, bf16[8,64,64]{2,1,0:T(8,128)(2,1)S(1)}, u32[]{:S(2)}, u32[]{:S(2)}) collective-permute-start(bf16[8,64,64]{2,1,0:T(8,128)(2,1)S(1)} %get-tuple-element.26), channel_id=1, source_target_pairs={{1,0},{2,1},{3,2},{4,3},{5,4},{6,5},{7,6},{8,7},{9,8},{10,9},{11,1... | collective-permute-start | bytes 196616 | tf_op jit(solution)/shard_map/ppermute | solution.py:334
  6.2 3.9 %collective-permute-start = (bf16[8,64,64]{2,1,0:T(8,128)(2,1)S(1)}, bf16[8,64,64]{2,1,0:T(8,128)(2,1)S(1)}, u32[]{:S(2)}, u32[]{:S(2)}) collective-permute-start(bf16[8,64,64]{2,1,0:T(8,128)(2,1)S(1)} %get-tuple-element.27), channel_id=1, source_target_pairs={{0,1},{1,2},{2,3},{3,4},{4,5},{5,6},{6,7},{7,8},{8,9},{9,10},{10,1... | collective-permute-start | bytes 196616 | tf_op jit(solution)/shard_map/ppermute | solution.py:333
  10.1 0.7 %collective-permute-done.1.high_in = bf16[8,64,64]{2,1,0:T(8,128)(2,1)S(1)} collective-permute-done((bf16[8,64,64]{2,1,0:T(8,128)(2,1)S(1)}, bf16[8,64,64]{2,1,0:T(8,128)(2,1)S(1)}, u32[]{:S(2)}, u32[]{:S(2)}) %collective-permute-start.1) | collective-permute-done | bytes 65568 | tf_op jit(solution)/shard_map/ppermute | solution.py:334
  10.9 1.2 %collective-permute-done.low_in = bf16[8,64,64]{2,1,0:T(8,128)(2,1)S(1)} collective-permute-done((bf16[8,64,64]{2,1,0:T(8,128)(2,1)S(1)}, bf16[8,64,64]{2,1,0:T(8,128)(2,1)S(1)}, u32[]{:S(2)}, u32[]{:S(2)}) %collective-permute-start) | collective-permute-done | bytes 65568 | tf_op jit(solution)/shard_map/ppermute | solution.py:333
  12.0 0.6 %copy-done.2 = bf16[8,64,64]{2,1,0:T(8,128)(2,1)} copy-done((bf16[8,64,64]{2,1,0:T(8,128)(2,1)}, bf16[8,64,64]{2,1,0:T(8,128)(2,1)S(1)}, u32[]{:S(2)}) %copy-start.2) | copy-done | bytes 65560
  12.7 9.4 %shard_map.103 = (bf16[8,512,64]{2,1,0:T(8,128)(2,1)}, f32[8,32,512]{2,1,0:T(8,128)}, bf16[8,8,512]{2,1,0:T(8,128)(2,1)}, bf16[8,8,512]{2,1,0:T(8,128)(2,1)}, s32[256,128]{1,0:T(8,128)}) custom-call(s32[8,27]{1,0:T(8,128)} %nb.5, bf16[8,512,64]{2,1,0:T(8,128)(2,1)} %copy-done, s32[8,16]{1,0:T(8,128)} %occ.1, bf16[8,64,64]{2,1,0:T(8,128)(2,1)} %copy-done.2, ...), custom_call_target="tpu_custom_call" | custom-call | tf_op jit(solution)/shard_map/pallas_call | solution.py:320
  22.1 5.2 %collective-permute-start.2 = (bf16[8,8,512]{2,1,0:T(8,128)(2,1)}, bf16[8,8,512]{2,1,0:T(8,128)(2,1)S(1)}, u32[]{:S(2)}, u32[]{:S(2)}) collective-permute-start(bf16[8,8,512]{2,1,0:T(8,128)(2,1)} %get-tuple-element.15), channel_id=1, source_target_pairs={{0,1},{1,2},{2,3},{3,4},{4,5},{5,6},{6,7},{7,8},{8,9},{9,10},{10,1... | collective-permute-start | bytes 196616 | tf_op jit(solution)/shard_map/ppermute | solution.py:333
  27.3 1.9 %collective-permute-start.3 = (bf16[8,8,512]{2,1,0:T(8,128)(2,1)}, bf16[8,8,512]{2,1,0:T(8,128)(2,1)S(1)}, u32[]{:S(2)}, u32[]{:S(2)}) collective-permute-start(bf16[8,8,512]{2,1,0:T(8,128)(2,1)} %get-tuple-element.16), channel_id=1, source_target_pairs={{1,0},{2,1},{3,2},{4,3},{5,4},{6,5},{7,6},{8,7},{9,8},{10,9},{11,1... | collective-permute-start | bytes 196616 | tf_op jit(solution)/shard_map/ppermute | solution.py:334
  29.3 4.7 %collective-permute-done.3.high_in = bf16[8,8,512]{2,1,0:T(8,128)(2,1)S(1)} collective-permute-done((bf16[8,8,512]{2,1,0:T(8,128)(2,1)}, bf16[8,8,512]{2,1,0:T(8,128)(2,1)S(1)}, u32[]{:S(2)}, u32[]{:S(2)}) %collective-permute-start.3) | collective-permute-done | bytes 65568 | tf_op jit(solution)/shard_map/ppermute | solution.py:334
  34.0 0.6 %copy-done.6 = bf16[8,8,512]{2,1,0:T(8,128)(2,1)} copy-done((bf16[8,8,512]{2,1,0:T(8,128)(2,1)}, bf16[8,8,512]{2,1,0:T(8,128)(2,1)S(1)}, u32[]{:S(2)}) %copy-start.6) | copy-done | bytes 65560
  34.6 5.1 %shard_map.104 = (bf16[8,64,128]{2,1,0:T(8,128)(2,1)}, f32[8,16,512]{2,1,0:T(8,128)}, bf16[8,8,512]{2,1,0:T(8,128)(2,1)}, bf16[8,8,512]{2,1,0:T(8,128)(2,1)}, s32[128,128]{1,0:T(8,128)}) custom-call(s32[8,27]{1,0:T(8,128)} %nb.5, f32[8,32,512]{2,1,0:T(8,128)} %get-tuple-element.14.own_in, bf16[8,8,512]{2,1,0:T(8,128)(2,1)} %copy-done.5, ...), custom_call_target="tpu_custom_call" | custom-call | tf_op jit(solution)/shard_map/pallas_call | solution.py:320
  39.7 2.0 %collective-permute-start.4 = (bf16[8,8,512]{2,1,0:T(8,128)(2,1)}, bf16[8,8,512]{2,1,0:T(8,128)(2,1)S(1)}, u32[]{:S(2)}, u32[]{:S(2)}) collective-permute-start(bf16[8,8,512]{2,1,0:T(8,128)(2,1)} %get-tuple-element.20), channel_id=1, source_target_pairs={{0,1},{1,2},{2,3},{3,4},{4,5},{5,6},{6,7},{7,8},{8,9},{9,10},{10,1... | collective-permute-start | bytes 196616 | tf_op jit(solution)/shard_map/ppermute | solution.py:333
  41.7 2.4 %collective-permute-start.5 = (bf16[8,8,512]{2,1,0:T(8,128)(2,1)}, bf16[8,8,512]{2,1,0:T(8,128)(2,1)S(1)}, u32[]{:S(2)}, u32[]{:S(2)}) collective-permute-start(bf16[8,8,512]{2,1,0:T(8,128)(2,1)} %get-tuple-element.21), channel_id=1, source_target_pairs={{1,0},{2,1},{3,2},{4,3},{5,4},{6,5},{7,6},{8,7},{9,8},{10,9},{11,1... | collective-permute-start | bytes 196616 | tf_op jit(solution)/shard_map/ppermute | solution.py:334
  44.1 2.3 %copy.14 = bf16[8,512,64]{1,2,0:T(8,128)(2,1)} copy(bf16[8,512,64]{2,1,0:T(8,128)(2,1)} %get-tuple-element.23) | data formatting | bytes 1048576
  46.4 2.0 %collective-permute-done.5.high_in = bf16[8,8,512]{2,1,0:T(8,128)(2,1)S(1)} collective-permute-done((bf16[8,8,512]{2,1,0:T(8,128)(2,1)}, bf16[8,8,512]{2,1,0:T(8,128)(2,1)S(1)}, u32[]{:S(2)}, u32[]{:S(2)}) %collective-permute-start.5) | collective-permute-done | bytes 65568 | tf_op jit(solution)/shard_map/ppermute | solution.py:334
  48.4 0.6 %copy-done.4 = bf16[8,8,512]{2,1,0:T(8,128)(2,1)} copy-done((bf16[8,8,512]{2,1,0:T(8,128)(2,1)}, bf16[8,8,512]{2,1,0:T(8,128)(2,1)S(1)}, u32[]{:S(2)}) %copy-start.4) | copy-done | bytes 65560
  49.0 4.6 %shard_map.105 = bf16[8,8,256]{2,1,0:T(8,128)(2,1)} custom-call(s32[8,27]{1,0:T(8,128)} %nb.5, f32[8,16,512]{2,1,0:T(8,128)} %get-tuple-element.19.own_in, bf16[8,8,512]{2,1,0:T(8,128)(2,1)} %copy-done.3, bf16[8,8,512]{2,1,0:T(8,128)(2,1)} %copy-done.4, s32[128,128]{1,0:T(8,128)} %get-tuple-element.22.bits, bf16[27,256,256]{2,1,0:T(8,128)(2,1)} %weights.5), custom_call_target="tpu_custom_call" | custom-call | tf_op jit(solution)/shard_map/pallas_call | solution.py:320
  (16 shorter events, 0.1 us)
Async XLA Ops:
  3.4 8.6 %copy-start = (bf16[8,512,64]{2,1,0:T(8,128)(2,1)}, bf16[8,512,64]{2,1,0:T(8,128)(2,1)S(1)}, u32[]{:S(2)}) copy-start(bf16[8,512,64]{2,1,0:T(8,128)(2,1)S(1)} %copy.13.feat) | copy-start | bytes 1572868
  3.6 7.2 %collective-permute-start.1 = (bf16[8,64,64]{2,1,0:T(8,128)(2,1)S(1)}, bf16[8,64,64]{2,1,0:T(8,128)(2,1)S(1)}, u32[]{:S(2)}, u32[]{:S(2)}) collective-permute-start(bf16[8,64,64]{2,1,0:T(8,128)(2,1)S(1)} %get-tuple-element.26), channel_id=1, source_target_pairs={{1,0},{2,1},{3,2},{4,3},{5,4},{6,5},{7,6},{8,7},{9,8},{10,9},{11,1... | collective-permute-start | bytes 196616 | tf_op jit(solution)/shard_map/ppermute | solution.py:334
  6.2 5.8 %collective-permute-start = (bf16[8,64,64]{2,1,0:T(8,128)(2,1)S(1)}, bf16[8,64,64]{2,1,0:T(8,128)(2,1)S(1)}, u32[]{:S(2)}, u32[]{:S(2)}) collective-permute-start(bf16[8,64,64]{2,1,0:T(8,128)(2,1)S(1)} %get-tuple-element.27), channel_id=1, source_target_pairs={{0,1},{1,2},{2,3},{3,4},{4,5},{5,6},{6,7},{7,8},{8,9},{9,10},{10,1... | collective-permute-start | bytes 196616 | tf_op jit(solution)/shard_map/ppermute | solution.py:333
  10.9 1.2 %copy-start.1 = (bf16[8,64,64]{2,1,0:T(8,128)(2,1)}, bf16[8,64,64]{2,1,0:T(8,128)(2,1)S(1)}, u32[]{:S(2)}) copy-start(bf16[8,64,64]{2,1,0:T(8,128)(2,1)S(1)} %collective-permute-done.1.high_in) | copy-start | bytes 196612
  12.0 0.7 %copy-start.2 = (bf16[8,64,64]{2,1,0:T(8,128)(2,1)}, bf16[8,64,64]{2,1,0:T(8,128)(2,1)S(1)}, u32[]{:S(2)}) copy-start(bf16[8,64,64]{2,1,0:T(8,128)(2,1)S(1)} %collective-permute-done.low_in) | copy-start | bytes 196612
  22.1 7.2 %collective-permute-start.2 = (bf16[8,8,512]{2,1,0:T(8,128)(2,1)}, bf16[8,8,512]{2,1,0:T(8,128)(2,1)S(1)}, u32[]{:S(2)}, u32[]{:S(2)}) collective-permute-start(bf16[8,8,512]{2,1,0:T(8,128)(2,1)} %get-tuple-element.15), channel_id=1, source_target_pairs={{0,1},{1,2},{2,3},{3,4},{4,5},{5,6},{6,7},{7,8},{8,9},{9,10},{10,1... | collective-permute-start | bytes 196616 | tf_op jit(solution)/shard_map/ppermute | solution.py:333
  27.3 6.7 %collective-permute-start.3 = (bf16[8,8,512]{2,1,0:T(8,128)(2,1)}, bf16[8,8,512]{2,1,0:T(8,128)(2,1)S(1)}, u32[]{:S(2)}, u32[]{:S(2)}) collective-permute-start(bf16[8,8,512]{2,1,0:T(8,128)(2,1)} %get-tuple-element.16), channel_id=1, source_target_pairs={{1,0},{2,1},{3,2},{4,3},{5,4},{6,5},{7,6},{8,7},{9,8},{10,9},{11,1... | collective-permute-start | bytes 196616 | tf_op jit(solution)/shard_map/ppermute | solution.py:334
  29.3 4.8 %copy-start.5 = (bf16[8,8,512]{2,1,0:T(8,128)(2,1)}, bf16[8,8,512]{2,1,0:T(8,128)(2,1)S(1)}, u32[]{:S(2)}) copy-start(bf16[8,8,512]{2,1,0:T(8,128)(2,1)S(1)} %collective-permute-done.2.low_in) | copy-start | bytes 196612
  34.0 0.6 %copy-start.6 = (bf16[8,8,512]{2,1,0:T(8,128)(2,1)}, bf16[8,8,512]{2,1,0:T(8,128)(2,1)S(1)}, u32[]{:S(2)}) copy-start(bf16[8,8,512]{2,1,0:T(8,128)(2,1)S(1)} %collective-permute-done.3.high_in) | copy-start | bytes 196612
  39.7 6.7 %collective-permute-start.4 = (bf16[8,8,512]{2,1,0:T(8,128)(2,1)}, bf16[8,8,512]{2,1,0:T(8,128)(2,1)S(1)}, u32[]{:S(2)}, u32[]{:S(2)}) collective-permute-start(bf16[8,8,512]{2,1,0:T(8,128)(2,1)} %get-tuple-element.20), channel_id=1, source_target_pairs={{0,1},{1,2},{2,3},{3,4},{4,5},{5,6},{6,7},{7,8},{8,9},{9,10},{10,1... | collective-permute-start | bytes 196616 | tf_op jit(solution)/shard_map/ppermute | solution.py:333
  41.7 6.7 %collective-permute-start.5 = (bf16[8,8,512]{2,1,0:T(8,128)(2,1)}, bf16[8,8,512]{2,1,0:T(8,128)(2,1)S(1)}, u32[]{:S(2)}, u32[]{:S(2)}) collective-permute-start(bf16[8,8,512]{2,1,0:T(8,128)(2,1)} %get-tuple-element.21), channel_id=1, source_target_pairs={{1,0},{2,1},{3,2},{4,3},{5,4},{6,5},{7,6},{8,7},{9,8},{10,9},{11,1... | collective-permute-start | bytes 196616 | tf_op jit(solution)/shard_map/ppermute | solution.py:334
  46.4 2.0 %copy-start.3 = (bf16[8,8,512]{2,1,0:T(8,128)(2,1)}, bf16[8,8,512]{2,1,0:T(8,128)(2,1)S(1)}, u32[]{:S(2)}) copy-start(bf16[8,8,512]{2,1,0:T(8,128)(2,1)S(1)} %collective-permute-done.4.low_in) | copy-start | bytes 196612
  48.4 0.6 %copy-start.4 = (bf16[8,8,512]{2,1,0:T(8,128)(2,1)}, bf16[8,8,512]{2,1,0:T(8,128)(2,1)S(1)}, u32[]{:S(2)}) copy-start(bf16[8,8,512]{2,1,0:T(8,128)(2,1)S(1)} %collective-permute-done.5.high_in) | copy-start | bytes 196612
where the time goes:
time: 54.1 us; the launch traced here: 53.6 us
  Pallas kernels  19.1 us (35%)
  starting transfers between devices  17.9 us (33%)
  waiting for transfers between devices  8.66 us (16%)
  local copies, waits for them, and re-layouts  6.98 us (13%)
  between operations  0.74 us (1%)
    pallas_call x3, Pallas kernels, call(): pl.pallas_call(body, out_shape=[jax.ShapeDtypeStruct(shape, dtype) for sh...  19.1 us
    ppermute x3, starting transfers between devices, exchange(): low = lax.ppermute(last, 'morton', forward)  11.1 us
    ppermute x3, waiting for transfers between devices, exchange(): high = lax.ppermute(first, 'morton', [(b, a) for a, b in forward])  7.48 us
    ppermute x3, starting transfers between devices, exchange(): high = lax.ppermute(first, 'morton', [(b, a) for a, b in forward])  6.86 us
    unnamed x16, local copies, waits for them, and re-layouts  5.76 us
    ppermute x3, waiting for transfers between devices, exchange(): low = lax.ppermute(last, 'morton', forward)  1.18 us
  transfers between devices with their start and end apart: 6, of which 4 were waited for; matrix products, arithmetic and copies ran while one was open for 4% of the time, Pallas kernels for 0%

commit v1 on v0

v1 whole, which is shorter than its diff:
```python
import jax
import jax.numpy as jnp
from jax import lax
from jax.experimental import pallas as pl
from jax.experimental.pallas import tpu as pltpu
from jax.sharding import PartitionSpec as P

BRICKS = 8
LANES = 512
F32 = jnp.float32
BF16 = jnp.bfloat16


def iota(shape, dim):
    return lax.broadcasted_iota(jnp.int32, shape, dim)


def band_pairs(source, band):
    @pl.loop(0, 9)
    def _(tap):
        minus, same, plus = (source[3 * tap + e] for e in range(3))
        zero = jnp.zeros_like(same)
        low = jnp.concatenate([same, minus], axis=1)
        high = jnp.concatenate([plus, same], axis=1)
        before = jnp.concatenate([minus, zero], axis=1)
        after = jnp.concatenate([zero, plus], axis=1)
        blank = jnp.zeros((64, 128), BF16)
        rows = (
            (blank, blank), (before, blank),
            (low, blank), (high, before),
            (after, low), (blank, high),
            (blank, after), (blank, blank),
        )
        for at, (left, right) in enumerate(rows):
            band[tap, at * 64 : at * 64 + 64, 0:128] = left
            band[tap, at * 64 : at * 64 + 64, 128:256] = right


def band_single(source, band):
    @pl.loop(0, 9)
    def _(tap):
        minus, same, plus = (source[3 * tap + e] for e in range(3))
        blank = jnp.zeros_like(same)
        rows = ((minus, blank), (same, minus), (plus, same), (blank, plus))
        for at, (left, right) in enumerate(rows):
            band[tap, at * 128 : at * 128 + 128, 0:128] = left
            band[tap, at * 128 : at * 128 + 128, 128:256] = right


def assemble(side, halo, nb, sources, cols):
    row = iota((8, LANES + 2 * halo), 0)

    def source(brick, tap):
        number = nb[brick, tap]
        return jnp.where(number < 0, BRICKS, lax.rem(number, BRICKS))

    @pl.loop(0, BRICKS // 2)
    def _(pair):
        for dx, ref in sources:
            index = [
                [[source(2 * pair + b, 9 * dx + 3 * dy + dz) for dz in range(3)] for dy in range(3)]
                for b in range(2)
            ]
            for plane in range(side if dx == 1 else 1):
                at = slice(8 * plane, 8 * plane + 8)
                shifted = [[], [], []]
                for b in range(2):
                    views = []
                    for dy in range(3):
                        before, here, after = index[b][dy]
                        views.append(
                            jnp.concatenate(
                                [
                                    ref[before, at, LANES - halo : LANES],
                                    ref[here, at, :],
                                    ref[after, at, 0:halo],
                                ],
                                axis=1,
                            )
                        )
                    back, mid, front = views
                    shifted[0].append(
                        jnp.where(
                            row == 0,
                            pltpu.roll(back, (9 - side) % 8, 0),
                            pltpu.roll(mid, 1, 0),
                        )
                    )
                    shifted[1].append(mid)
                    shifted[2].append(
                        jnp.where(
                            row == side - 1,
                            pltpu.roll(front, side - 1, 0),
                            pltpu.roll(mid, 7, 0),
                        )
                    )
                to = plane + 1 if dx == 1 else (0 if dx == 0 else side + 1)
                rows = pl.ds(pl.multiple_of(16 * pair, 16), 16)
                for c in range(3):
                    cols[c, to, rows, :] = jnp.concatenate(shifted[c], axis=0).astype(BF16)


def convolve(side, depth, cols, weights, finish):
    chunk = min(side, 4)
    matrix = jnp.concatenate([weights(tap) for tap in range(9)], axis=0)
    for half in range(2):
        lanes = slice(256 * half, 256 * half + depth)
        for first in range(0, side, chunk):
            left = jnp.concatenate(
                [
                    cols[c, first + a : first + a + chunk, :, lanes].reshape(chunk * 64, depth)
                    for a in range(3)
                    for c in range(3)
                ],
                axis=1,
            )
            sums = jnp.dot(left, matrix, preferred_element_type=F32)
            finish(half, first, sums.reshape(chunk, BRICKS, 8, 256))


def rounded(value):
    return value.astype(BF16).astype(F32)


def pool_bits(bits, fine_side, temp, pooled):
    half = fine_side // 2
    count = BRICKS * half * 8
    joined = bits[0 : BRICKS * fine_side * 8, :].reshape(BRICKS * half, 2, 8, 128)
    temp[0:count, :] = (joined[:, 0] | joined[:, 1]).reshape(count, 128)
    temp[count : count + 16, :] = jnp.zeros((16, 128), jnp.int32)
    for at in range(BRICKS * half):
        even = temp[pl.ds(8 * at, 8, stride=2), :]
        odd = temp[pl.ds(8 * at + 1, 8, stride=2), :]
        pooled[8 * at : 8 * at + 8, :] = even | odd


def reduce_level(side, block, fine, kernel, bits, bit_width, emit):
    half = side // 2
    width = 2 * block
    for at in range(LANES // width):
        parts = []
        for ci in range(2):
            for cj in range(2):
                pieces = []
                for lane in range(at * width, (at + 1) * width, 128):
                    pieces.append(
                        jnp.concatenate(
                            [
                                fine[lane // 128, pl.ds((b * side + 2 * i + ci) * 8 + cj, 8, stride=2), :]
                                for b in range(BRICKS)
                                for i in range(half)
                            ],
                            axis=0,
                        )
                    )
                parts += pieces
        left = jnp.concatenate(parts, axis=1).astype(BF16)
        sums = jnp.dot(left, kernel, preferred_element_type=F32)
        mask = ((bits[0 : BRICKS * half * 8, :] >> (bit_width * at)) & ((1 << bit_width) - 1)) != 0
        wide = sums.shape[1]
        for lane in range(0, wide, 128):
            emit(
                at * wide + lane,
                jnp.where(mask, jnp.maximum(sums[:, lane : lane + 128], 0.0), 0.0),
            )


def relayout(temp, lane):
    for q in range(4):
        even = temp[pl.ds(2 * q, 64, stride=8), :]
        odd = temp[pl.ds(2 * q + 1, 64, stride=8), :]
        yield q, jnp.where(lane < 64, even, pltpu.roll(odd, 64, 1))


def fused(nb, feat, occ, conv_one, kernel_one, conv_two_hbm, kernel_two_hbm, conv_three_hbm,
          out_one, out_two, out_three,
          own_one, own_two, own_three, low, high, cols_one, cols_two, cols_three,
          band_one, band_two, conv_two, kernel_two, conv_three,
          fine, temp, wide, wide_three, bits_one, bits_two, bits_three, bits_temp,
          outgoing, incoming, load_sems, send_sems, recv_sems):
    me = lax.axis_index("morton")
    count = lax.axis_size("morton")
    has_low, has_high = me > 0, me < count - 1
    sides = ((has_low, me - 1), (has_high, me + 1))

    loads = [
        pltpu.make_async_copy(source, target, load_sems.at[at])
        for at, (source, target) in enumerate(
            ((conv_two_hbm, conv_two), (kernel_two_hbm, kernel_two), (conv_three_hbm, conv_three))
        )
    ]
    for load in loads:
        load.start()

    barrier = pltpu.get_barrier_semaphore()
    for there, device in sides:
        @pl.when(there)
        def _():
            pl.semaphore_signal(barrier, inc=1, device_id={"morton": device},
                                device_id_type=pl.DeviceIdType.MESH)

    def transfer(level, to):
        return pltpu.make_async_remote_copy(
            src_ref=outgoing.at[level, to],
            dst_ref=incoming.at[level, 1 - to],
            send_sem=send_sems.at[level, to],
            recv_sem=recv_sems.at[level, 1 - to],
            device_id={"morton": sides[to][1]},
            device_id_type=pl.DeviceIdType.MESH,
        )

    def send(level):
        for to in range(2):
            @pl.when(sides[to][0])
            def _():
                transfer(level, to).start()

    def receive(level):
        for source in range(2):
            @pl.when(sides[source][0])
            def _():
                transfer(level, 1 - source).wait_recv()
                (low, high)[source][0:BRICKS] = incoming[level, source].astype(F32)

    lane = iota((64, 128), 1)
    row = iota((64, 16), 0)
    column = iota((64, 16), 1)
    upper = (lane >= 64).astype(jnp.int32)
    for ref in (own_one, own_two, own_three):
        ref[BRICKS] = jnp.zeros(ref.shape[1:], F32)
    for ref in (low, high):
        ref[...] = jnp.zeros(ref.shape, F32)

    @pl.loop(0, BRICKS)
    def _(b):
        words = jnp.broadcast_to(occ[pl.ds(b, 1), :], (64, 16))
        octet = (words >> (8 * (row % 4))) & 255
        picked = jnp.where(column == row // 4, octet.astype(F32), 0.0)
        mask = jnp.broadcast_to(jnp.sum(picked, axis=1, keepdims=True), (64, 128)).astype(jnp.int32)
        bits_one[pl.ds(pl.multiple_of(64 * b, 64), 64), :] = mask
        temp[:, 0:64] = feat[b].astype(F32)
        for q, both in relayout(temp, lane):
            value = jnp.where(((mask >> (2 * q + upper)) & 1) != 0, both, 0.0)
            lanes = slice(128 * q, 128 * q + 128)
            own_one[b, :, lanes] = value
            outgoing[0, 0, b, :, lanes] = value[0:8].astype(BF16)
            outgoing[0, 1, b, :, lanes] = value[56:64].astype(BF16)

    pl.semaphore_wait(barrier, jnp.minimum(me, 1) + jnp.minimum(count - 1 - me, 1))
    send(0)
    band_pairs(conv_one, band_one)
    assemble(8, 128, nb, ((1, own_one),), cols_one)
    loads[0].wait()
    band_single(conv_two, band_two)
    receive(0)
    assemble(8, 128, nb, ((0, low), (2, high)), cols_one)

    small_upper = (iota((8, 128), 1) >= 64).astype(jnp.int32)

    def finish_one(half, first, sums):
        for p in range(sums.shape[0]):
            for b in range(BRICKS):
                at = b * 64 + (first + p) * 8
                mask = bits_one[at : at + 8, :]
                for part in range(2):
                    q = 2 * half + part
                    fine[q, at : at + 8, :] = rounded(
                        jnp.where(
                            ((mask >> (2 * q + small_upper)) & 1) != 0,
                            jnp.maximum(sums[p, b, :, 128 * part : 128 * part + 128], 0.0),
                            0.0,
                        )
                    )

    convolve(8, 512, cols_one, lambda tap: band_one[tap], finish_one)
    fine[:, 512:528, :] = jnp.zeros((4, 16, 128), F32)
    pool_bits(bits_one, 8, bits_temp, bits_two)

    def emit_into(own, level, planes):
        def emit(lane_at, value):
            value = rounded(value).reshape(BRICKS, 8 * planes, 128)
            lanes = slice(lane_at, lane_at + 128)
            own[0:BRICKS, :, lanes] = value
            outgoing[level, 0, :, :, lanes] = value[:, 0:8].astype(BF16)
            outgoing[level, 1, :, :, lanes] = value[:, 8 * planes - 8 :].astype(BF16)
        return emit

    reduce_level(8, 64, fine, kernel_one[...], bits_two, 2, emit_into(own_two, 1, 4))
    send(1)
    assemble(4, 128, nb, ((1, own_two),), cols_two)

    @pl.loop(0, BRICKS)
    def _(b):
        for q in range(4):
            both = fine[q, pl.ds(pl.multiple_of(64 * b, 64), 64), :]
            wide[pl.ds(2 * q, 64, stride=8), :] = both
            wide[pl.ds(2 * q + 1, 64, stride=8), :] = pltpu.roll(both, 64, 1)
        out_one[b] = wide[:, 0:64].astype(BF16)

    receive(1)
    assemble(4, 128, nb, ((0, low), (2, high)), cols_two)

    def finish_two(half, first, sums):
        for p in range(sums.shape[0]):
            for b in range(BRICKS):
                at = b * 32 + (first + p) * 8
                mask = bits_two[at : at + 8, :]
                for part in range(2):
                    q = 2 * half + part
                    fine[q, at : at + 8, :] = rounded(
                        jnp.where(
                            ((mask >> (2 * q)) & 3) != 0,
                            jnp.maximum(sums[p, b, :, 128 * part : 128 * part + 128], 0.0),
                            0.0,
                        )
                    )

    convolve(4, 512, cols_two, lambda tap: band_two[tap], finish_two)
    pool_bits(bits_two, 4, bits_temp, bits_three)
    loads[1].wait()
    reduce_level(4, 128, fine, kernel_two[...], bits_three, 4, emit_into(own_three, 2, 2))
    send(2)
    assemble(2, 256, nb, ((1, own_three),), cols_three)
    for b in range(BRICKS):
        for i in range(4):
            for k in range(4):
                at = b * 32 + 8 * i
                wide[pl.ds(64 * b + 16 * i + k, 4, stride=4), :] = fine[k, at : at + 4, :]
    out_two[...] = wide[...].reshape(BRICKS, 64, 128).astype(BF16)
    loads[2].wait()
    receive(2)
    assemble(2, 256, nb, ((0, low), (2, high)), cols_three)

    def finish_three(half, first, sums):
        for p in range(sums.shape[0]):
            for b in range(BRICKS):
                at = b * 16 + (first + p) * 8
                mask = ((bits_three[at : at + 8, :] >> (4 * half)) & 15) != 0
                for part in range(2):
                    value = jnp.where(
                        mask, jnp.maximum(sums[p, b, :, 128 * part : 128 * part + 128], 0.0), 0.0
                    )
                    wide_three[part, pl.ds(8 * b + 4 * (first + p) + half, 2, stride=2), :] = value[0:2]

    convolve(2, 768, cols_three, lambda tap: conv_three[3 * tap : 3 * tap + 3].reshape(768, 256), finish_three)
    for part in range(2):
        out_three[:, :, 128 * part : 128 * part + 128] = (
            wide_three[part].reshape(BRICKS, 8, 128).astype(BF16)
        )
    for level in range(3):
        for to in range(2):
            @pl.when(sides[to][0])
            def _():
                transfer(level, to).wait_send()


def on_device(features, neighbours, occupancy, conv_one, first_reduce_kernel,
              conv_two, second_reduce_kernel, conv_three):
    vm = pl.BlockSpec(memory_space=pltpu.VMEM)
    hbm = pl.BlockSpec(memory_space=pl.ANY)
    kernel_two = second_reduce_kernel.reshape(1024, 256)
    scratch = [
        ((BRICKS + 1, 64, LANES), F32), ((BRICKS + 1, 32, LANES), F32),
        ((BRICKS + 1, 16, LANES), F32), ((BRICKS + 1, 8, LANES), F32),
        ((BRICKS + 1, 8, LANES), F32),
        ((3, 10, 64, 768), BF16), ((3, 6, 64, 768), BF16), ((3, 4, 64, 1024), BF16),
        ((9, 512, 256), BF16), ((9, 512, 256), BF16),
        (conv_two.shape, BF16), (kernel_two.shape, BF16), (conv_three.shape, BF16),
        ((4, 528, 128), F32), ((512, 128), F32), ((512, 128), F32), ((2, 64, 128), F32),
        ((512, 128), jnp.int32), ((256, 128), jnp.int32), ((128, 128), jnp.int32),
        ((272, 128), jnp.int32),
        ((3, 2, BRICKS, 8, LANES), BF16), ((3, 2, BRICKS, 8, LANES), BF16),
    ]
    return pl.pallas_call(
        fused,
        out_shape=[
            jax.ShapeDtypeStruct((BRICKS, 512, 64), BF16),
            jax.ShapeDtypeStruct((BRICKS, 64, 128), BF16),
            jax.ShapeDtypeStruct((BRICKS, 8, 256), BF16),
        ],
        in_specs=[pl.BlockSpec(memory_space=pltpu.SMEM), vm, vm, vm, vm, hbm, hbm, hbm],
        out_specs=[vm, vm, vm],
        scratch_shapes=[pltpu.VMEM(shape, dtype) for shape, dtype in scratch]
        + [pltpu.SemaphoreType.DMA((3,)), pltpu.SemaphoreType.DMA((3, 2)),
           pltpu.SemaphoreType.DMA((3, 2))],
        compiler_params=pltpu.CompilerParams(
            collective_id=0, has_side_effects=True, vmem_limit_bytes=56 << 20
        ),
    )(neighbours, features, occupancy, conv_one, first_reduce_kernel.reshape(512, 128),
      conv_two, kernel_two, conv_three)


def solution(mesh):
    split = P(("tiles", "morton"), None, None)
    flat = P(("tiles", "morton"), None)
    return jax.shard_map(
        on_device,
        mesh=mesh,
        in_specs=(split, flat, flat, P(), P(), P(), P(), P()),
        out_specs=(split, split, split),
        check_vma=False,
    )
```

time: 54.1 us -> 30 us (0.55)
  starting transfers between devices: 17.9 us -> 0 us
  waiting for transfers between devices: 8.66 us -> 0 us
  Pallas kernels: 19.1 us -> 21.2 us
  local copies, waits for them, and re-layouts: 6.98 us -> 7.66 us
    ppermute x6 -> x0, starting transfers between devices: 17.9 us -> none  [the longest x3 11.1 us: exchange(): low = lax.ppermute(last, 'morton', forward)]
    ppermute x6 -> x0, waiting for transfers between devices: 8.66 us -> none  [the longest x3 7.48 us: exchange(): high = lax.ppermute(first, 'morton', [(b, a) for a, b in forward])]
    pallas_call x0 -> x1, local copies, waits for them, and re-layouts: none -> 2.34 us  [on_device(): pl.pallas_call(fused, out_shape=[jax.ShapeDtypeStruct((BRICKS, 512, 64),...]
    pallas_call x3 -> x1, Pallas kernels: 19.1 us -> 21.2 us  [on_device(): pl.pallas_call(fused, out_shape=[jax.ShapeDtypeStruct((BRICKS, 512, 64),...]
    slice x1 -> x0, local copies, waits for them, and re-layouts: 0.83 us -> none  [masked_plane(): words = occupancy[:, 2 * plane:2 * plane + 2]]
    unnamed x16 -> x3, local copies, waits for them, and re-layouts: 5.76 us -> 5.31 us
  transfers between devices with their start and end apart: 6 -> 0, of which waited for: 4 -> 0; matrix products, arithmetic and copies ran while one was open for 4% -> 0% of each run, Pallas kernels for 0% -> 0%
where the time goes in v1:
time: 30 us; the launch traced here: 29.5 us
  Pallas kernels  21.2 us (71%)
  local copies, waits for them, and re-layouts  7.66 us (26%)
  between operations  0.64 us (2%)
    pallas_call x1, Pallas kernels, on_device(): pl.pallas_call(fused, out_shape=[jax.ShapeDtypeStruct((BRICKS, 512, 64),...  21.2 us
    unnamed x3, local copies, waits for them, and re-layouts  5.31 us
    pallas_call x1, local copies, waits for them, and re-layouts, on_device(): pl.pallas_call(fused, out_shape=[jax.ShapeDtypeStruct((BRICKS, 512, 64),...  2.34 us

profile of v1, /device:TPU:7, one launch (start us, length us, event | category | flops | bytes accessed | tf_op | source)
XLA Modules:
  0.0 29.5 jit_solution(4443356879177820170)
XLA Ops:
  0.6 2.4 %copy.11.feat = bf16[8,512,64]{2,1,0:T(8,128)(2,1)} copy(bf16[8,512,64]{1,2,0:T(8,128)(2,1)} %param.8) | data formatting | bytes 1048576 | tf_op args[0]
  3.0 21.2 %shard_map.103 = (bf16[8,512,64]{2,1,0:T(8,128)(2,1)}, bf16[8,64,128]{2,1,0:T(8,128)(2,1)}, bf16[8,8,256]{2,1,0:T(8,128)(2,1)}) custom-call(s32[8,27]{1,0:T(8,128)} %nb.1, bf16[8,512,64]{2,1,0:T(8,128)(2,1)} %copy.11.feat, s32[8,16]{1,0:T(8,128)} %occ.1, bf16[27,64,64]{2,1,0:T(8,128)(2,1)} %conv_one.1, bf16[512,128]{1,0:T(8,128)(2,1)} %bitcast.3, ...), custom_call_target="tpu_custom_call" | custom-call | tf_op jit(solution)/shard_map/pallas_call | solution.py:374
  24.2 2.3 %copy.12 = bf16[8,512,64]{1,2,0:T(8,128)(2,1)} copy(bf16[8,512,64]{2,1,0:T(8,128)(2,1)} %get-tuple-element.3) | data formatting | bytes 1048576 | tf_op jit(solution)/shard_map/pallas_call | solution.py:374
  26.6 1.6 %copy.15 = bf16[8,64,128]{2,1,0:T(8,128)(2,1)} copy(bf16[8,64,128]{2,1,0:T(8,128)(2,1)} %get-tuple-element.10) | data formatting | bytes 262144
  28.2 1.4 %copy.16 = bf16[8,8,256]{2,1,0:T(8,128)(2,1)} copy(bf16[8,8,256]{2,1,0:T(8,128)(2,1)} %get-tuple-element.11) | data formatting | bytes 65536

commit v2 on v1

--- a/solution.py
+++ b/solution.py
@@ -238,7 +238,7 @@
         picked = jnp.where(column == row // 4, octet.astype(F32), 0.0)
         mask = jnp.broadcast_to(jnp.sum(picked, axis=1, keepdims=True), (64, 128)).astype(jnp.int32)
         bits_one[pl.ds(pl.multiple_of(64 * b, 64), 64), :] = mask
-        temp[:, 0:64] = feat[b].astype(F32)
+        temp[:, 0:64] = feat[b].astype(F32).T
         for q, both in relayout(temp, lane):
             value = jnp.where(((mask >> (2 * q + upper)) & 1) != 0, both, 0.0)
             lanes = slice(128 * q, 128 * q + 128)
@@ -295,7 +295,7 @@
             both = fine[q, pl.ds(pl.multiple_of(64 * b, 64), 64), :]
             wide[pl.ds(2 * q, 64, stride=8), :] = both
             wide[pl.ds(2 * q + 1, 64, stride=8), :] = pltpu.roll(both, 64, 1)
-        out_one[b] = wide[:, 0:64].astype(BF16)
+        out_one[b] = wide[:, 0:64].T.astype(BF16)
 
     receive(1)
     assemble(4, 128, nb, ((0, low), (2, high)), cols_two)
@@ -371,10 +371,10 @@
         ((272, 128), jnp.int32),
         ((3, 2, BRICKS, 8, LANES), BF16), ((3, 2, BRICKS, 8, LANES), BF16),
     ]
-    return pl.pallas_call(
+    first, second, third = pl.pallas_call(
         fused,
         out_shape=[
-            jax.ShapeDtypeStruct((BRICKS, 512, 64), BF16),
+            jax.ShapeDtypeStruct((BRICKS, 64, 512), BF16),
             jax.ShapeDtypeStruct((BRICKS, 64, 128), BF16),
             jax.ShapeDtypeStruct((BRICKS, 8, 256), BF16),
         ],
@@ -386,8 +386,9 @@
         compiler_params=pltpu.CompilerParams(
             collective_id=0, has_side_effects=True, vmem_limit_bytes=56 << 20
         ),
-    )(neighbours, features, occupancy, conv_one, first_reduce_kernel.reshape(512, 128),
+    )(neighbours, jnp.swapaxes(features, 1, 2), occupancy, conv_one, first_reduce_kernel.reshape(512, 128),
       conv_two, kernel_two, conv_three)
+    return jnp.swapaxes(first, 1, 2), second, third
 
 
 def solution(mesh):

time: 30 us -> 27.2 us (0.907)
  local copies, waits for them, and re-layouts: 7.66 us -> 4.81 us
  Pallas kernels: 21.2 us -> 21.5 us
    pallas_call x1 -> x0, local copies, waits for them, and re-layouts: 2.34 us -> none  [on_device(): pl.pallas_call(fused, out_shape=[jax.ShapeDtypeStruct((BRICKS, 512, 64),...]
    unnamed x3, local copies, waits for them, and re-layouts: 5.31 us -> 4.81 us
where the time goes in v2:
time: 27.2 us; the launch traced here: 26.9 us
  Pallas kernels  21.5 us (79%)
  local copies, waits for them, and re-layouts  4.81 us (18%)
  between operations  0.64 us (2%)
    pallas_call x1, Pallas kernels, on_device(): pl.pallas_call(fused, out_shape=[jax.ShapeDtypeStruct((BRICKS, 64, 512),...  21.5 us
    unnamed x3, local copies, waits for them, and re-layouts  4.81 us

profile of v2, /device:TPU:7, one launch (start us, length us, event | category | flops | bytes accessed | tf_op | source)
XLA Modules:
  0.0 26.9 jit_solution(11813043706964536145)
XLA Ops:
  0.6 21.5 %shard_map.103 = (bf16[8,64,512]{2,1,0:T(8,128)(2,1)}, bf16[8,64,128]{2,1,0:T(8,128)(2,1)}, bf16[8,8,256]{2,1,0:T(8,128)(2,1)}) custom-call(s32[8,27]{1,0:T(8,128)} %nb.1, bf16[8,64,512]{2,1,0:T(8,128)(2,1)} %bitcast.4, s32[8,16]{1,0:T(8,128)} %occ.1, bf16[27,64,64]{2,1,0:T(8,128)(2,1)} %conv_one.1, bf16[512,128]{1,0:T(8,128)(2,1)} %bitcast.7, ...), custom_call_target="tpu_custom_call" | custom-call | tf_op jit(solution)/shard_map/pallas_call | solution.py:374
  22.1 1.9 %copy.14 = bf16[8,512,64]{1,2,0:T(8,128)(2,1)} copy(bf16[8,512,64]{1,2,0:T(8,128)(2,1)} %bitcast.6) | data formatting | bytes 1048576
  24.0 1.6 %copy.15 = bf16[8,64,128]{2,1,0:T(8,128)(2,1)} copy(bf16[8,64,128]{2,1,0:T(8,128)(2,1)} %get-tuple-element.13) | data formatting | bytes 262144
  25.6 1.4 %copy.16 = bf16[8,8,256]{2,1,0:T(8,128)(2,1)} copy(bf16[8,8,256]{2,1,0:T(8,128)(2,1)} %get-tuple-element.14) | data formatting | bytes 65536

commit v3 on v2

--- a/solution.py
+++ b/solution.py
@@ -173,10 +173,10 @@
 
 
 def fused(nb, feat, occ, conv_one, kernel_one, conv_two_hbm, kernel_two_hbm, conv_three_hbm,
-          out_one, out_two, out_three,
-          own_one, own_two, own_three, low, high, cols_one, cols_two, cols_three,
-          band_one, band_two, conv_two, kernel_two, conv_three,
-          fine, temp, wide, wide_three, bits_one, bits_two, bits_three, bits_temp,
+          out_one, out_two, cols_three, bits_three, conv_three,
+          own_one, own_two, own_three, low, high, cols_one, cols_two,
+          band_one, band_two, conv_two, kernel_two,
+          fine, temp, wide, bits_one, bits_two, bits_temp,
           outgoing, incoming, load_sems, send_sems, recv_sems):
     me = lax.axis_index("morton")
     count = lax.axis_size("morton")
@@ -327,9 +327,21 @@
                 at = b * 32 + 8 * i
                 wide[pl.ds(64 * b + 16 * i + k, 4, stride=4), :] = fine[k, at : at + 4, :]
     out_two[...] = wide[...].reshape(BRICKS, 64, 128).astype(BF16)
-    loads[2].wait()
     receive(2)
     assemble(2, 256, nb, ((0, low), (2, high)), cols_three)
+
+    loads[2].wait()
+    for level in range(3):
+        for to in range(2):
+            @pl.when(sides[to][0])
+            def _():
+                transfer(level, to).wait_send()
+
+
+def last_level(one, two, cols_three, bits_three, conv_three,
+               out_one, out_two, out_three, wide_three):
+    out_one[...] = one[...]
+    out_two[...] = two[...]
 
     def finish_three(half, first, sums):
         for p in range(sums.shape[0]):
@@ -347,47 +359,55 @@
         out_three[:, :, 128 * part : 128 * part + 128] = (
             wide_three[part].reshape(BRICKS, 8, 128).astype(BF16)
         )
-    for level in range(3):
-        for to in range(2):
-            @pl.when(sides[to][0])
-            def _():
-                transfer(level, to).wait_send()
 
 
 def on_device(features, neighbours, occupancy, conv_one, first_reduce_kernel,
               conv_two, second_reduce_kernel, conv_three):
     vm = pl.BlockSpec(memory_space=pltpu.VMEM)
-    hbm = pl.BlockSpec(memory_space=pl.ANY)
+    hbm = pl.BlockSpec(memory_space=pltpu.HBM)
     kernel_two = second_reduce_kernel.reshape(1024, 256)
     scratch = [
         ((BRICKS + 1, 64, LANES), F32), ((BRICKS + 1, 32, LANES), F32),
         ((BRICKS + 1, 16, LANES), F32), ((BRICKS + 1, 8, LANES), F32),
         ((BRICKS + 1, 8, LANES), F32),
-        ((3, 10, 64, 768), BF16), ((3, 6, 64, 768), BF16), ((3, 4, 64, 1024), BF16),
+        ((3, 10, 64, 768), BF16), ((3, 6, 64, 768), BF16),
         ((9, 512, 256), BF16), ((9, 512, 256), BF16),
-        (conv_two.shape, BF16), (kernel_two.shape, BF16), (conv_three.shape, BF16),
-        ((4, 528, 128), F32), ((512, 128), F32), ((512, 128), F32), ((2, 64, 128), F32),
-        ((512, 128), jnp.int32), ((256, 128), jnp.int32), ((128, 128), jnp.int32),
+        (conv_two.shape, BF16), (kernel_two.shape, BF16),
+        ((4, 528, 128), F32), ((512, 128), F32), ((512, 128), F32),
+        ((512, 128), jnp.int32), ((256, 128), jnp.int32),
         ((272, 128), jnp.int32),
         ((3, 2, BRICKS, 8, LANES), BF16), ((3, 2, BRICKS, 8, LANES), BF16),
     ]
-    first, second, third = pl.pallas_call(
+    shapes = [
+        jax.ShapeDtypeStruct((BRICKS, 64, 512), BF16),
+        jax.ShapeDtypeStruct((BRICKS, 64, 128), BF16),
+    ]
+    first, second, cols, bits, weights = pl.pallas_call(
         fused,
-        out_shape=[
-            jax.ShapeDtypeStruct((BRICKS, 64, 512), BF16),
-            jax.ShapeDtypeStruct((BRICKS, 64, 128), BF16),
-            jax.ShapeDtypeStruct((BRICKS, 8, 256), BF16),
+        out_shape=shapes
+        + [
+            jax.ShapeDtypeStruct((3, 4, 64, 1024), BF16),
+            jax.ShapeDtypeStruct((128, 128), jnp.int32),
+            jax.ShapeDtypeStruct(conv_three.shape, BF16),
         ],
         in_specs=[pl.BlockSpec(memory_space=pltpu.SMEM), vm, vm, vm, vm, hbm, hbm, hbm],
-        out_specs=[vm, vm, vm],
+        out_specs=[vm] * 5,
         scratch_shapes=[pltpu.VMEM(shape, dtype) for shape, dtype in scratch]
         + [pltpu.SemaphoreType.DMA((3,)), pltpu.SemaphoreType.DMA((3, 2)),
            pltpu.SemaphoreType.DMA((3, 2))],
         compiler_params=pltpu.CompilerParams(
-            collective_id=0, has_side_effects=True, vmem_limit_bytes=56 << 20
+            collective_id=0, has_side_effects=True, vmem_limit_bytes=36 << 20
         ),
-    )(neighbours, jnp.swapaxes(features, 1, 2), occupancy, conv_one, first_reduce_kernel.reshape(512, 128),
-      conv_two, kernel_two, conv_three)
+    )(neighbours, jnp.swapaxes(features, 1, 2), occupancy, conv_one,
+      first_reduce_kernel.reshape(512, 128), conv_two, kernel_two, conv_three)
+    first, second, third = pl.pallas_call(
+        last_level,
+        out_shape=shapes + [jax.ShapeDtypeStruct((BRICKS, 8, 256), BF16)],
+        in_specs=[vm] * 5,
+        out_specs=[vm] * 3,
+        scratch_shapes=[pltpu.VMEM((2, 64, 128), F32)],
+        compiler_params=pltpu.CompilerParams(vmem_limit_bytes=16 << 20),
+    )(first, second, cols, bits, weights)
     return jnp.swapaxes(first, 1, 2), second, third
 
 

time: 27.2 us -> 31 us (1.14)
  local copies, waits for them, and re-layouts: 4.81 us -> 8.53 us
    unnamed x3 -> x16, local copies, waits for them, and re-layouts: 4.81 us -> 8.53 us
    pallas_call x1 -> x2, Pallas kernels: 21.5 us -> 21.4 us  [the longest x1 19.6 us: on_device(): pl.pallas_call(fused, out_shape=shapes + [jax.ShapeDtypeStruct((3, 4, 64,...]
where the time goes in v3:
time: 31 us; the launch traced here: 30.6 us
  Pallas kernels  21.4 us (69%)
  local copies, waits for them, and re-layouts  8.53 us (28%)
  between operations  0.66 us (2%)
    pallas_call x1, Pallas kernels, on_device(): pl.pallas_call(fused, out_shape=shapes + [jax.ShapeDtypeStruct((3, 4, 64,...  19.6 us
    unnamed x16, local copies, waits for them, and re-layouts  8.53 us
    pallas_call x1, Pallas kernels, on_device(): pl.pallas_call(last_level, out_shape=shapes + [jax.ShapeDtypeStruct((BRIC...  1.81 us

profile of v3, /device:TPU:7, one launch (start us, length us, event | category | flops | bytes accessed | tf_op | source)
XLA Modules:
  0.0 30.6 jit_solution(5320228522190548669)
XLA Ops:
  0.6 0.0 copy-start
  0.6 2.0 %copy-done = bf16[27,256,256]{2,1,0:T(8,128)(2,1)S(1)} copy-done((bf16[27,256,256]{2,1,0:T(8,128)(2,1)S(1)}, bf16[27,256,256]{2,1,0:T(8,128)(2,1)}, u32[]{:S(2)}) %copy-start) | copy-done | bytes 3538968
  2.6 0.0 copy-start.1
  2.6 1.2 %copy-done.1 = bf16[27,128,128]{2,1,0:T(8,128)(2,1)S(1)} copy-done((bf16[27,128,128]{2,1,0:T(8,128)(2,1)S(1)}, bf16[27,128,128]{2,1,0:T(8,128)(2,1)}, u32[]{:S(2)}) %copy-start.1) | copy-done | bytes 884760
  3.8 0.0 copy-start.2
  3.8 1.0 %copy-done.2 = bf16[8,512,64]{1,2,0:T(8,128)(2,1)S(1)} copy-done((bf16[8,512,64]{1,2,0:T(8,128)(2,1)S(1)}, bf16[8,512,64]{1,2,0:T(8,128)(2,1)}, u32[]{:S(2)}) %copy-start.2) | copy-done | bytes 524312
  4.8 0.0 copy-start.3
  4.8 1.0 %copy-done.3 = bf16[8,128,256]{2,1,0:T(8,128)(2,1)S(1)} copy-done((bf16[8,128,256]{2,1,0:T(8,128)(2,1)S(1)}, bf16[8,128,256]{2,1,0:T(8,128)(2,1)}, u32[]{:S(2)}) %copy-start.3) | copy-done | bytes 524312
  5.9 0.0 copy-start.4
  5.9 1.0 %copy-done.4 = bf16[27,64,64]{2,1,0:T(8,128)(2,1)S(1)} copy-done((bf16[27,64,64]{2,1,0:T(8,128)(2,1)S(1)}, bf16[27,64,64]{2,1,0:T(8,128)(2,1)}, u32[]{:S(2)}) %copy-start.4) | copy-done | bytes 221208
  6.9 0.0 copy-start.5
  6.9 0.9 %copy-done.5 = bf16[8,64,128]{2,1,0:T(8,128)(2,1)S(1)} copy-done((bf16[8,64,128]{2,1,0:T(8,128)(2,1)S(1)}, bf16[8,64,128]{2,1,0:T(8,128)(2,1)}, u32[]{:S(2)}) %copy-start.5) | copy-done | bytes 131096
  7.8 0.0 copy-start.6
  7.8 0.7 %copy-done.6 = s32[8,27]{1,0:T(8,128)S(1)} copy-done((s32[8,27]{1,0:T(8,128)S(1)}, s32[8,27]{1,0:T(8,128)}, u32[]{:S(2)}) %copy-start.6) | copy-done | bytes 888
  8.5 0.0 copy-start.7
  8.5 0.7 %copy-done.7 = s32[8,16]{1,0:T(8,128)S(1)} copy-done((s32[8,16]{1,0:T(8,128)S(1)}, s32[8,16]{1,0:T(8,128)}, u32[]{:S(2)}) %copy-start.7) | copy-done | bytes 536
  9.2 19.6 %shard_map.103 = (bf16[8,64,512]{2,1,0:T(8,128)(2,1)S(1)}, bf16[8,64,128]{2,1,0:T(8,128)(2,1)S(1)}, bf16[3,4,64,1024]{3,2,1,0:T(8,128)(2,1)S(1)}, s32[128,128]{1,0:T(8,128)S(1)}, bf16[27,256,256]{2,1,0:T(8,128)(2,1)S(1)}) custom-call(s32[8,27]{1,0:T(8,128)S(1)} %copy-done.6, bf16[8,64,512]{2,1,0:T(8,128)(2,1)S(1)} %bitcast.4, s32[8,16]{1,0:T(8,128)S(1)} %copy-done.7, ...), custom_call_target="tpu_custom_call" | custom-call | tf_op jit(solution)/shard_map/pallas_call | solution.py:385
  28.7 1.8 %shard_map.104 = (bf16[8,64,512]{2,1,0:T(8,128)(2,1)}, bf16[8,64,128]{2,1,0:T(8,128)(2,1)}, bf16[8,8,256]{2,1,0:T(8,128)(2,1)}) custom-call(bf16[8,64,512]{2,1,0:T(8,128)(2,1)S(1)} %get-tuple-element.11.one, bf16[8,64,128]{2,1,0:T(8,128)(2,1)S(1)} %get-tuple-element.12.two, bf16[3,4,64,1024]{3,2,1,0:T(8,128)(2,1)S(1)} %get-tuple-element.13.cols_three, ...), custom_call_target="tpu_custom_call" | custom-call | tf_op jit(solution)/shard_map/pallas_call | solution.py:403
Async XLA Ops:
  0.6 2.0 %copy-start = (bf16[27,256,256]{2,1,0:T(8,128)(2,1)S(1)}, bf16[27,256,256]{2,1,0:T(8,128)(2,1)}, u32[]{:S(2)}) copy-start(bf16[27,256,256]{2,1,0:T(8,128)(2,1)} %conv_three_hbm.1) | copy-start | bytes 10616836
  2.6 1.2 %copy-start.1 = (bf16[27,128,128]{2,1,0:T(8,128)(2,1)S(1)}, bf16[27,128,128]{2,1,0:T(8,128)(2,1)}, u32[]{:S(2)}) copy-start(bf16[27,128,128]{2,1,0:T(8,128)(2,1)} %conv_two_hbm.1) | copy-start | bytes 2654212
  3.8 1.0 %copy-start.2 = (bf16[8,512,64]{1,2,0:T(8,128)(2,1)S(1)}, bf16[8,512,64]{1,2,0:T(8,128)(2,1)}, u32[]{:S(2)}) copy-start(bf16[8,512,64]{1,2,0:T(8,128)(2,1)} %param.8) | copy-start | bytes 1572868
  4.8 1.0 %copy-start.3 = (bf16[8,128,256]{2,1,0:T(8,128)(2,1)S(1)}, bf16[8,128,256]{2,1,0:T(8,128)(2,1)}, u32[]{:S(2)}) copy-start(bf16[8,128,256]{2,1,0:T(8,128)(2,1)} %param.14) | copy-start | bytes 1572868
  5.9 1.0 %copy-start.4 = (bf16[27,64,64]{2,1,0:T(8,128)(2,1)S(1)}, bf16[27,64,64]{2,1,0:T(8,128)(2,1)}, u32[]{:S(2)}) copy-start(bf16[27,64,64]{2,1,0:T(8,128)(2,1)} %conv_one.1) | copy-start | bytes 663556
  6.9 0.9 %copy-start.5 = (bf16[8,64,128]{2,1,0:T(8,128)(2,1)S(1)}, bf16[8,64,128]{2,1,0:T(8,128)(2,1)}, u32[]{:S(2)}) copy-start(bf16[8,64,128]{2,1,0:T(8,128)(2,1)} %param.12) | copy-start | bytes 393220
  7.8 0.7 %copy-start.6 = (s32[8,27]{1,0:T(8,128)S(1)}, s32[8,27]{1,0:T(8,128)}, u32[]{:S(2)}) copy-start(s32[8,27]{1,0:T(8,128)} %nb.1) | copy-start | bytes 2596
  8.5 0.7 %copy-start.7 = (s32[8,16]{1,0:T(8,128)S(1)}, s32[8,16]{1,0:T(8,128)}, u32[]{:S(2)}) copy-start(s32[8,16]{1,0:T(8,128)} %occ.1) | copy-start | bytes 1540

commit v4 on v3

--- a/solution.py
+++ b/solution.py
@@ -398,8 +398,11 @@
         compiler_params=pltpu.CompilerParams(
             collective_id=0, has_side_effects=True, vmem_limit_bytes=36 << 20
         ),
-    )(neighbours, jnp.swapaxes(features, 1, 2), occupancy, conv_one,
-      first_reduce_kernel.reshape(512, 128), conv_two, kernel_two, conv_three)
+    )(*(
+        pltpu.with_memory_space_constraint(x, pltpu.HBM)
+        for x in (neighbours, jnp.swapaxes(features, 1, 2), occupancy, conv_one,
+                  first_reduce_kernel.reshape(512, 128), conv_two, kernel_two, conv_three)
+    ))
     first, second, third = pl.pallas_call(
         last_level,
         out_shape=shapes + [jax.ShapeDtypeStruct((BRICKS, 8, 256), BF16)],

time: 31 us -> 22.2 us (0.72)
  local copies, waits for them, and re-layouts: 8.53 us -> 0 us
    unnamed x16 -> x0, local copies, waits for them, and re-layouts: 8.53 us -> none
where the time goes in v4:
time: 22.2 us; the launch traced here: 22 us
  Pallas kernels  21.4 us (96%)
  between operations  0.64 us (3%)
    pallas_call x1, Pallas kernels, on_device(): pl.pallas_call(fused, out_shape=shapes + [jax.ShapeDtypeStruct((3, 4, 64,...  19.6 us
    pallas_call x1, Pallas kernels, on_device(): pl.pallas_call(last_level, out_shape=shapes + [jax.ShapeDtypeStruct((BRIC...  1.82 us

profile of v4, /device:TPU:7, one launch (start us, length us, event | category | flops | bytes accessed | tf_op | source)
XLA Modules:
  0.0 22.0 jit_solution(9352615177896249546)
XLA Ops:
  0.6 19.6 %shard_map.103 = (bf16[8,64,512]{2,1,0:T(8,128)(2,1)S(1)}, bf16[8,64,128]{2,1,0:T(8,128)(2,1)S(1)}, bf16[3,4,64,1024]{3,2,1,0:T(8,128)(2,1)S(1)}, s32[128,128]{1,0:T(8,128)S(1)}, bf16[27,256,256]{2,1,0:T(8,128)(2,1)S(1)}) custom-call(s32[8,27]{1,0:T(8,128)} %nb.1, bf16[8,64,512]{2,1,0:T(8,128)(2,1)} %bitcast.4, s32[8,16]{1,0:T(8,128)} %occ.1, ...), custom_call_target="tpu_custom_call" | custom-call | tf_op jit(solution)/shard_map/pallas_call | solution.py:385
  20.2 1.8 %shard_map.104 = (bf16[8,64,512]{2,1,0:T(8,128)(2,1)}, bf16[8,64,128]{2,1,0:T(8,128)(2,1)}, bf16[8,8,256]{2,1,0:T(8,128)(2,1)}) custom-call(bf16[8,64,512]{2,1,0:T(8,128)(2,1)S(1)} %get-tuple-element.11.one, bf16[8,64,128]{2,1,0:T(8,128)(2,1)S(1)} %get-tuple-element.12.two, bf16[3,4,64,1024]{3,2,1,0:T(8,128)(2,1)S(1)} %get-tuple-element.13.cols_three, ...), custom_call_target="tpu_custom_call" | custom-call | tf_op jit(solution)/shard_map/pallas_call | solution.py:406
